TPU v7x, 32 devices: a whole 2x2x4 slice. The times are simulated.
32 devices in a mesh: tilt: 2 (over y), dom: 16 (over z, x, core).
Axes of the slice: x: 2, y: 2, z: 4, core: 2. Of those that a mesh axis runs over, the one named last changes fastest.
Arguments:
- sections: bfloat16 [32, 256, 256], P('dom'), may hold values from -6 to 6
- images: bfloat16 [32, 4, 256, 256], P('dom', 'tilt'), may hold values from -6 to 6
- slice_rows: bfloat16 [4, 256, 256], P('tilt'), may hold values from -0.375 to 0.375
- slice_cols: bfloat16 [4, 256, 256], P('tilt'), may hold values from -0.375 to 0.375
- ctf_filter: bfloat16 [4, 256, 256], P('tilt'), may hold values from -0.375 to 0.375
- nbr_owner: int32 [32, 2, 8], P('dom'), may hold values from 0 to 15, all different within a row; in each aligned block of 4 rows (0 to 3, 4 to 7, ..., all dimensions but the last counted through in order) at most 4 rows name the same one
- nbr_local: int32 [32, 16], P('dom'), may hold values from 0 to 1
- nbr_side: int32 [32, 16], P('dom'), may hold values from 0 to 1
- nbr_weight: float32 [32, 16], P('dom'), may hold values from 0.25 to 2
Outputs:
- section_grad: float32 [32, 256, 256], P('dom', 'tilt')
- scores: float32 [32], P('dom')
Inputs may be any that keep to these rules, and one draw needn't show every extreme that they name: `nbr_owner`: among the 32 neighbour entries of one spatial block's particles, at most 4 name the same owner block; some blocks reach 4.
All inputs are finite; a program needn't handle non-finite values.
Results may differ from a plain program's by a relative error of at most 0.013.
Values may be sent and summed in bfloat16 or wider, within the bound.
No kernel may reach another device: no remote copies, remote signals or barrier semaphores. Data moves between devices by JAX's collectives and lax.ppermute only.
A program may use at most 64 MiB of HBM per device.

v0:
```python
import jax
import jax.numpy as jnp
from jax import lax
from jax.sharding import PartitionSpec as P

OVL = 16


def split_dot(weights, bands):
    hi = weights.astype(jnp.bfloat16)
    rest = weights - hi.astype(jnp.float32)
    mid = rest.astype(jnp.bfloat16)
    low = (rest - mid.astype(jnp.float32)).astype(jnp.bfloat16)
    total = jnp.dot(hi, bands, preferred_element_type=jnp.float32)
    total = total + jnp.dot(mid, bands, preferred_element_type=jnp.float32)
    return total + jnp.dot(low, bands, preferred_element_type=jnp.float32)


def on_device(
    sections, images, slice_rows, slice_cols, ctf_filter, nbr_owner, nbr_local, nbr_side, nbr_weight
):
    own_count = sections.shape[0]
    pixels = sections.shape[1]
    tilt_count = images.shape[1]
    neighbours = nbr_local.shape[1]
    peer_count = lax.axis_size("dom")
    total = own_count * peer_count
    me = lax.axis_index("dom")
    band_size = tilt_count * OVL * pixels
    target = nbr_owner.reshape(own_count, neighbours) * own_count + nbr_local
    every = jnp.arange(total)
    hits = target[:, :, None] == every[None, None, :]
    fwd = [
        jnp.sum(jnp.where(hits & (nbr_side == s)[:, :, None], nbr_weight[:, :, None], 0.0), axis=1)
        for s in (0, 1)
    ]
    target_all = lax.all_gather(target, "dom", axis=0, tiled=True)
    side_all = lax.all_gather(nbr_side, "dom", axis=0, tiled=True)
    weight_all = lax.all_gather(nbr_weight, "dom", axis=0, tiled=True)
    halfway = jnp.einsum(
        "kij,tlj->ktil", sections, slice_cols, preferred_element_type=jnp.float32
    ).astype(jnp.bfloat16)
    projected = jnp.einsum(
        "tai,ktil->ktal", slice_rows, halfway, preferred_element_type=jnp.float32
    ).astype(jnp.bfloat16)
    edges = jnp.stack((projected[:, :, :OVL], projected[:, :, pixels - OVL :]), axis=1)
    edges_all = lax.all_gather(edges, "dom", axis=0, tiled=True)
    lower_part = split_dot(fwd[0], edges_all[:, 0].reshape(total, band_size))
    upper_part = split_dot(fwd[1], edges_all[:, 1].reshape(total, band_size))
    lower_part = lower_part.reshape(own_count, tilt_count, OVL, pixels)
    upper_part = upper_part.reshape(own_count, tilt_count, OVL, pixels)
    residual = images.astype(jnp.float32) - projected.astype(jnp.float32)
    residual = residual.at[:, :, :OVL].add(-upper_part)
    residual = residual.at[:, :, pixels - OVL :].add(-lower_part)
    residual_portion = residual.astype(jnp.bfloat16)
    smoothed_images = jnp.einsum(
        "tab,ktbc->ktac", ctf_filter, residual_portion, preferred_element_type=jnp.float32
    ).astype(jnp.bfloat16)
    filtered_images = jnp.einsum(
        "ktac,tdc->ktad", smoothed_images, ctf_filter, preferred_element_type=jnp.float32
    )
    score_part = jnp.sum(filtered_images * filtered_images, axis=(1, 2, 3))
    tilt_groups = lax.axis_size("tilt")
    scores = 0.5 * lax.psum(score_part, "tilt") / (tilt_count * tilt_groups * pixels * pixels)
    filtered_portion = filtered_images.astype(jnp.bfloat16)
    reverse_pass = jnp.einsum(
        "tab,ktac->ktbc", ctf_filter, filtered_portion, preferred_element_type=jnp.float32
    ).astype(jnp.bfloat16)
    weighted = jnp.einsum(
        "ktbc,tcd->ktbd", reverse_pass, ctf_filter, preferred_element_type=jnp.float32
    ).astype(jnp.bfloat16)
    grad_bands = jnp.stack((weighted[:, :, :OVL], weighted[:, :, pixels - OVL :]), axis=1)
    grad_all = lax.all_gather(grad_bands, "dom", axis=0, tiled=True)
    mine = me * own_count + jnp.arange(own_count)
    named = target_all[None, :, :] == mine[:, None, None]
    back = [
        jnp.sum(jnp.where(named & (side_all == s)[None], weight_all[None], 0.0), axis=2)
        for s in (0, 1)
    ]
    add_top = split_dot(back[0], grad_all[:, 1].reshape(total, band_size))
    add_bottom = split_dot(back[1], grad_all[:, 0].reshape(total, band_size))
    add_top = add_top.reshape(own_count, tilt_count, OVL, pixels)
    add_bottom = add_bottom.reshape(own_count, tilt_count, OVL, pixels)
    proj_grad = weighted.astype(jnp.float32)
    proj_grad = proj_grad.at[:, :, :OVL].add(add_top)
    proj_grad = proj_grad.at[:, :, pixels - OVL :].add(add_bottom)
    proj_half = proj_grad.astype(jnp.bfloat16)
    upward = jnp.einsum(
        "tai,ktal->ktil", slice_rows, proj_half, preferred_element_type=jnp.float32
    ).astype(jnp.bfloat16)
    partial_grad = -jnp.einsum(
        "ktil,tlj->kij", upward, slice_cols, preferred_element_type=jnp.float32
    )
    section_grad = lax.psum_scatter(partial_grad, "tilt", scatter_dimension=1, tiled=True)
    return (section_grad, scores)


def solution(mesh):
    in_specs = (
        P("dom", None, None),
        P("dom", "tilt", None, None),
        P("tilt", None, None),
        P("tilt", None, None),
        P("tilt", None, None),
        P("dom", None, None),
        P("dom", None),
        P("dom", None),
        P("dom", None),
    )
    out_specs = (P("dom", "tilt", None), P("dom"))
    return jax.shard_map(
        on_device, mesh=mesh, in_specs=in_specs, out_specs=out_specs, check_vma=False
    )
```

profile of v0, /device:TPU:0, one launch (start us, length us, event | category | flops | bytes accessed | tf_op | source)
XLA Modules:
  0.0 136.8 jit_solution(1483881849874437)
XLA Ops:
  7.2 1.9 %convert_subtract_fusion = (f32[2,2,256,256]{3,2,0,1:T(8,128)S(1)}, bf16[2,2,256,256]{3,2,0,1:T(8,128)(2,1)S(1)}) fusion(bf16[2,2,256,256]{3,2,1,0:T(8,128)(2,1)} %param.18, bf16[2,256,256]{2,1,0:T(8,128)(2,1)} %param.19, bf16[2,256,256]{2,1,0:T(8,128)(2,1)} %param.20, bf16[2,256,256]{2,1,0:T(8,128)(2,1)} %param.17), kind=kOutput, calls=%fused_computation.26 | convolution fusion | flops 269746176 | bytes 2883584 | tf_op jit(solution)/shard_map/tai,ktil->ktal/dot_general | solution.py:43
  9.1 0.6 pad_maximum_fusion
  9.8 0.6 copy-done.5
  10.5 0.6 copy-done.6
  11.1 0.7 copy-done.4
  11.8 0.7 copy-done.3
  12.6 38.9 %all-gather.6.cloned.1.call-done = bf16[32,2,2,16,256]{4,3,0,2,1:T(8,128)(2,1)} async-done(((bf16[2,2,2,16,256]{4,3,0,2,1:T(8,128)(2,1)}), bf16[32,2,2,16,256]{4,3,0,2,1:T(8,128)(2,1)}) %all-gather.6.cloned.1.call-update) | async-done | bytes 1048592 | tf_op jit(solution)/shard_map/all_gather | solution.py:47
  51.5 1.3 fusion.53
  52.8 0.2 reshape_squeeze.12
  53.2 0.2 convolution_add_fusion.7
  53.4 0.2 fusion.1
  53.7 0.2 reshape_squeeze.13
  54.1 0.2 convolution_add_fusion.5
  54.3 0.2 fusion
  54.6 0.7 multiply_reduce_fusion
  55.3 0.6 fusion.58
  55.9 0.6 pad_maximum_fusion.1
  56.7 19.3 %all-gather.2 = f32[16,2,16]{2,1,0:T(2,128)S(1)} all-gather(f32[1,2,16]{2,1,0:T(2,128)S(1)} %bitcast.146), channel_id=1, replica_groups=mesh['tilt'=2,'dom'=16] {'dom'}, dimensions={0}, use_global_device_ids=true | all-gather | bytes 2176 | tf_op jit(solution)/shard_map/all_gather | solution.py:39
  76.1 17.4 %all-gather = s32[16,2,16]{2,1,0:T(2,128)S(1)} all-gather(s32[1,2,16]{2,1,0:T(2,128)S(1)} %bitcast.145), channel_id=1, replica_groups=mesh['tilt'=2,'dom'=16] {'dom'}, dimensions={0}, use_global_device_ids=true | all-gather | bytes 2176 | tf_op jit(solution)/shard_map/all_gather | solution.py:37
  93.5 18.8 %all-gather.1 = s32[16,2,16]{2,1,0:T(2,128)S(1)} all-gather(s32[1,2,16]{2,1,0:T(2,128)S(1)} %bitcast.147), channel_id=1, replica_groups=mesh['tilt'=2,'dom'=16] {'dom'}, dimensions={0}, use_global_device_ids=true | all-gather | bytes 2176 | tf_op jit(solution)/shard_map/all_gather | solution.py:38
  112.7 1.3 fusion.52
  114.0 0.2 reshape_squeeze.14
  114.5 0.2 convolution_add_fusion.3
  114.7 0.2 convolution_add_fusion.2
  114.9 0.2 reshape_squeeze.15
  115.4 0.2 convolution_add_fusion.1
  115.6 0.2 convolution_add_fusion
  115.9 0.9 copy-done.1
  116.8 1.5 %fusion.9 = f32[2,256,256]{2,1,0:T(8,128)} fusion(bf16[2,256,256]{2,1,0:T(8,128)(2,1)S(1)} %copy-done.1, bf16[2,256,256]{2,1,0:T(8,128)(2,1)S(1)} %copy-done.2, f32[2,2,256,256]{3,2,0,1:T(8,128)S(1)} %fusion.30), kind=kOutput, calls=%fused_computation.24 | convolution fusion | flops 269090816 | bytes 2097152 | tf_op jit(solution)/shard_map/ktil,tlj->kij/dot_general | solution.py:91
  118.3 4.9 %psum.7 = f32[2]{0:T(128)S(1)} all-reduce(f32[2]{0:T(128)S(1)} %get-tuple-element.70), channel_id=1, replica_groups=mesh['tilt'=2,'dom'=16] {'tilt'}, use_global_device_ids=true, to_apply=%region_6.7 | all-reduce | flops 2 | bytes 16 | tf_op jit(solution)/shard_map/psum | solution.py:64
  123.3 0.5 broadcast_multiply_fusion.1
  123.8 6.5 %reduce-scatter.2.cloned.1.call-done = f32[2,128,256]{2,1,0:T(8,128)} async-done(((f32[2,256,256]{2,1,0:T(8,128)}), f32[2,128,256]{2,1,0:T(8,128)}) %reduce-scatter.2.cloned.1.call-update) | async-done | bytes 262160 | tf_op jit(solution)/shard_map/reduce_scatter | solution.py:94
  (48 shorter events, 2.0 us)
Async XLA Ops:
  7.2 47.4 %copy-start = (bf16[2,256,256]{2,1,0:T(8,128)(2,1)S(1)}, bf16[2,256,256]{2,1,0:T(8,128)(2,1)}, u32[]{:S(2)}) copy-start(bf16[2,256,256]{2,1,0:T(8,128)(2,1)} %param.21) | copy-start | bytes 786436
  7.2 44.3 %all-gather.6.cloned.1.call-start = ((), (), s32[]{:S(2)}) async-start(), calls=%async_computation.1 | async-start | bytes 1114112 | tf_op jit(solution)/shard_map/all_gather | solution.py:47
  9.7 0.7 copy-start.5
  9.8 102.9 %all-gather.8.cloned.1.call-start = ((), (), s32[]{:S(2)}) async-start(), calls=%async_computation.2 | async-start | bytes 1114112 | tf_op jit(solution)/shard_map/all_gather | solution.py:73
  10.4 0.7 copy-start.6
  11.1 0.7 copy-start.4
  11.8 0.7 copy-start.3
  56.6 73.7 %reduce-scatter.2.cloned.1.call-start = ((), (), s32[]{:S(2)}) async-start(), calls=%async_computation.3 | async-start | bytes 786432 | tf_op jit(solution)/shard_map/reduce_scatter | solution.py:94
  115.8 1.0 copy-start.1
  115.8 1.0 copy-start.2
Sparse Core Ops, SparseCore 0:
  10.8 40.6 all-gather.5
  56.7 36.8 all-gather.7
  118.5 11.8 reduce-scatter.1
where the time goes:
time: 137 us
  blocking collectives  60.5 us (44%)
  waiting for transfers between devices  45.5 us (33%)
  between operations  14 us (10%)
  local copies, waits for them, and re-layouts  7.73 us (6%)
  matrix products  6.92 us (5%)
  other arithmetic  2.08 us (2%)
    all_gather x1, waiting for transfers between devices, on_device(): edges_all = lax.all_gather(edges, 'dom', axis=0, tiled=True)  38.9 us
    all_gather x1, blocking collectives, on_device(): weight_all = lax.all_gather(nbr_weight, 'dom', axis=0, tiled=True)  19.3 us
    all_gather x1, blocking collectives, on_device(): side_all = lax.all_gather(nbr_side, 'dom', axis=0, tiled=True)  18.8 us
    all_gather x1, blocking collectives, on_device(): target_all = lax.all_gather(target, 'dom', axis=0, tiled=True)  17.4 us
    reduce_scatter x1, waiting for transfers between devices, on_device(): lax.psum_scatter(partial_grad, 'tilt', scatter_dimension=1, tiled=True)  6.51 us
    psum x1, blocking collectives, on_device(): lax.psum(score_part, 'tilt')  4.94 us
    unnamed x20, local copies, waits for them, and re-layouts  3.68 us
  transfers between devices with their start and end apart: 3, of which 2 were waited for; matrix products, arithmetic and copies ran while one was open for 1% of the time, Pallas kernels for 0%

commit v1 on v0

--- a/solution.py
+++ b/solution.py
@@ -35,8 +35,11 @@
         for s in (0, 1)
     ]
     target_all = lax.all_gather(target, "dom", axis=0, tiled=True)
-    side_all = lax.all_gather(nbr_side, "dom", axis=0, tiled=True)
-    weight_all = lax.all_gather(nbr_weight, "dom", axis=0, tiled=True)
+    side_all, weight_all = jnp.split(
+        lax.all_gather(jnp.concatenate([nbr_side, nbr_weight], axis=1), "dom", axis=0, tiled=True),
+        [nbr_side.shape[1]],
+        axis=1,
+    )
     halfway = jnp.einsum(
         "kij,tlj->ktil", sections, slice_cols, preferred_element_type=jnp.float32
     ).astype(jnp.bfloat16)

time: 137 us -> 120 us (0.88)
  blocking collectives: 60.5 us -> 41.7 us
  waiting for transfers between devices: 45.5 us -> 46.9 us
    all_gather x2 -> x1, blocking collectives: 38.1 us -> 19.3 us  [on_device(): lax.all_gather(jnp.concatenate([nbr_side, nbr_weight], axis=1), 'dom', ax...]
    reduce_scatter x1, waiting for transfers between devices: 6.51 us -> 7.94 us  [on_device(): lax.psum_scatter(partial_grad, 'tilt', scatter_dimension=1, tiled=True)]
where the time goes in v1:
time: 120 us; the launch traced here: 119 us
  waiting for transfers between devices  46.9 us (39%)
  blocking collectives  41.7 us (35%)
  between operations  14 us (12%)
  local copies, waits for them, and re-layouts  7.66 us (6%)
  matrix products  6.92 us (6%)
  other arithmetic  2.15 us (2%)
    all_gather x1, waiting for transfers between devices, on_device(): edges_all = lax.all_gather(edges, 'dom', axis=0, tiled=True)  38.9 us
    all_gather x1, blocking collectives, on_device(): lax.all_gather(jnp.concatenate([nbr_side, nbr_weight], axis=1), 'dom', ax...  19.3 us
    all_gather x1, blocking collectives, on_device(): target_all = lax.all_gather(target, 'dom', axis=0, tiled=True)  17.4 us
    reduce_scatter x1, waiting for transfers between devices, on_device(): lax.psum_scatter(partial_grad, 'tilt', scatter_dimension=1, tiled=True)  7.94 us
    psum x1, blocking collectives, on_device(): lax.psum(score_part, 'tilt')  4.94 us
    unnamed x20, local copies, waits for them, and re-layouts  3.68 us
  transfers between devices with their start and end apart: 3, of which 2 were waited for; matrix products, arithmetic and copies ran while one was open for 1% of the time, Pallas kernels for 0%

profile of v1, /device:TPU:0, one launch (start us, length us, event | category | flops | bytes accessed | tf_op | source)
XLA Modules:
  0.0 119.5 jit_solution(6900480966023531452)
XLA Ops:
  7.2 1.9 %convert_subtract_fusion = (f32[2,2,256,256]{3,2,0,1:T(8,128)S(1)}, bf16[2,2,256,256]{3,2,0,1:T(8,128)(2,1)S(1)}) fusion(bf16[2,2,256,256]{3,2,1,0:T(8,128)(2,1)} %param.18, bf16[2,256,256]{2,1,0:T(8,128)(2,1)} %param.19, bf16[2,256,256]{2,1,0:T(8,128)(2,1)} %param.20, bf16[2,256,256]{2,1,0:T(8,128)(2,1)} %param.17), kind=kOutput, calls=%fused_computation.26 | convolution fusion | flops 269746176 | bytes 2883584 | tf_op jit(solution)/shard_map/tai,ktil->ktal/dot_general | solution.py:46
  9.1 0.6 pad_maximum_fusion
  9.8 0.6 copy-done.5
  10.5 0.6 copy-done.6
  11.1 0.7 copy-done.4
  11.8 0.7 copy-done.3
  12.6 38.9 %all-gather.5.cloned.1.call-done = bf16[32,2,2,16,256]{4,3,0,2,1:T(8,128)(2,1)} async-done(((bf16[2,2,2,16,256]{4,3,0,2,1:T(8,128)(2,1)}), bf16[32,2,2,16,256]{4,3,0,2,1:T(8,128)(2,1)}) %all-gather.5.cloned.1.call-update) | async-done | bytes 1048592 | tf_op jit(solution)/shard_map/all_gather | solution.py:50
  51.5 1.3 %fusion.53 = (bf16[32,1,2,16,256]{4,3,0,2,1:T(8,128)(2,1)S(1)}, bf16[32,1,2,16,256]{4,3,0,2,1:T(8,128)(2,1)S(1)}) fusion(bf16[32,2,2,16,256]{4,3,0,2,1:T(8,128)(2,1)} %all-gather.5.cloned.1.call-done), kind=kLoop, calls=%fused_computation.90 | loop fusion | bytes 2097152 | tf_op jit(solution)/shard_map/slice | solution.py:51
  52.8 0.2 reshape_squeeze.12
  53.1 0.2 fusion.37
  53.2 0.2 convolution_add_fusion.7
  53.4 0.2 fusion.1
  53.7 0.2 reshape_squeeze.13
  54.1 0.2 convolution_add_fusion.5
  54.3 0.2 fusion
  54.6 0.7 multiply_reduce_fusion
  55.3 0.6 fusion.59
  55.9 0.6 pad_maximum_fusion.1
  56.7 19.3 %all-gather.1 = f32[16,2,32]{2,1,0:T(2,128)S(1)} all-gather(f32[1,2,32]{2,1,0:T(2,128)S(1)} %maximum_bitcast_fusion), channel_id=1, replica_groups=mesh['tilt'=2,'dom'=16] {'dom'}, dimensions={0}, use_global_device_ids=true | all-gather | bytes 4352 | tf_op jit(solution)/shard_map/all_gather | solution.py:39
  76.2 17.4 %all-gather = s32[16,2,16]{2,1,0:T(2,128)S(1)} all-gather(s32[1,2,16]{2,1,0:T(2,128)S(1)} %bitcast.145), channel_id=1, replica_groups=mesh['tilt'=2,'dom'=16] {'dom'}, dimensions={0}, use_global_device_ids=true | all-gather | bytes 2176 | tf_op jit(solution)/shard_map/all_gather | solution.py:37
  93.9 1.3 %fusion.52 = (bf16[32,1,2,16,256]{4,3,0,2,1:T(8,128)(2,1)S(1)}, bf16[32,1,2,16,256]{4,3,0,2,1:T(8,128)(2,1)S(1)}) fusion(bf16[32,2,2,16,256]{4,3,0,2,1:T(8,128)(2,1)} %all-gather.7.cloned.1.call-done), kind=kLoop, calls=%fused_computation.89 | loop fusion | bytes 2097152 | tf_op jit(solution)/shard_map/slice | solution.py:84
  95.2 0.2 reshape_squeeze.14
  95.7 0.2 convolution_add_fusion.3
  95.9 0.2 convolution_add_fusion.2
  96.1 0.2 reshape_squeeze.15
  96.6 0.2 convolution_add_fusion.1
  96.8 0.2 convolution_add_fusion
  97.0 0.9 copy-done.1
  98.0 1.5 %fusion.9 = f32[2,256,256]{2,1,0:T(8,128)} fusion(bf16[2,256,256]{2,1,0:T(8,128)(2,1)S(1)} %copy-done.1, bf16[2,256,256]{2,1,0:T(8,128)(2,1)S(1)} %copy-done.2, f32[2,2,256,256]{3,2,0,1:T(8,128)S(1)} %fusion.30), kind=kOutput, calls=%fused_computation.24 | convolution fusion | flops 269090816 | bytes 2097152 | tf_op jit(solution)/shard_map/ktil,tlj->kij/dot_general | solution.py:94
  99.5 4.9 %psum.7 = f32[2]{0:T(128)S(1)} all-reduce(f32[2]{0:T(128)S(1)} %get-tuple-element.72), channel_id=1, replica_groups=mesh['tilt'=2,'dom'=16] {'tilt'}, use_global_device_ids=true, to_apply=%region_6.7 | all-reduce | flops 2 | bytes 16 | tf_op jit(solution)/shard_map/psum | solution.py:67
  104.5 0.5 broadcast_multiply_fusion.1
  105.0 7.9 %reduce-scatter.2.cloned.1.call-done = f32[2,128,256]{2,1,0:T(8,128)} async-done(((f32[2,256,256]{2,1,0:T(8,128)}), f32[2,128,256]{2,1,0:T(8,128)}) %reduce-scatter.2.cloned.1.call-update) | async-done | bytes 262160 | tf_op jit(solution)/shard_map/reduce_scatter | solution.py:97
  (47 shorter events, 1.8 us)
Async XLA Ops:
  7.2 47.4 %copy-start = (bf16[2,256,256]{2,1,0:T(8,128)(2,1)S(1)}, bf16[2,256,256]{2,1,0:T(8,128)(2,1)}, u32[]{:S(2)}) copy-start(bf16[2,256,256]{2,1,0:T(8,128)(2,1)} %param.21) | copy-start | bytes 786436
  7.2 44.3 %all-gather.5.cloned.1.call-start = ((), (), s32[]{:S(2)}) async-start(), calls=%async_computation.1 | async-start | bytes 1114112 | tf_op jit(solution)/shard_map/all_gather | solution.py:50
  9.7 0.7 copy-start.5
  9.8 84.1 %all-gather.7.cloned.1.call-start = ((), (), s32[]{:S(2)}) async-start(), calls=%async_computation.2 | async-start | bytes 1114112 | tf_op jit(solution)/shard_map/all_gather | solution.py:76
  10.4 0.7 copy-start.6
  11.1 0.7 copy-start.4
  11.8 0.7 copy-start.3
  56.6 56.3 %reduce-scatter.2.cloned.1.call-start = ((), (), s32[]{:S(2)}) async-start(), calls=%async_computation.3 | async-start | bytes 786432 | tf_op jit(solution)/shard_map/reduce_scatter | solution.py:97
  97.0 1.0 copy-start.1
  97.0 1.0 copy-start.2
Sparse Core Ops, SparseCore 0:
  10.8 40.6 all-gather.4
  56.7 36.8 all-gather.6
  99.7 13.2 reduce-scatter.1
